TPU v7x, 512 devices: a whole 4x8x8 slice. The times are simulated.
512 devices in a mesh: row: 256 (over y, x, z), col: 2 (over core).
Axes of the slice: x: 4, y: 8, z: 8, core: 2. Of those that a mesh axis runs over, the one named last changes fastest.
Arguments:
- panel: float32 [131072, 2048], P('row', 'col'), may hold values from -6 to 6
- inner_vecs: float32 [256, 4, 256, 128], P('row', None, 'col'), may hold values from -0.375 to 0.375
- inner_factor: float32 [256, 4, 128, 128], P('row'), may hold values from -0.5 to 0.5
- border_vecs: float32 [256, 4, 256, 128], P('row', None, 'col'), may hold values from -0.375 to 0.375
- border_factor: float32 [256, 4, 128, 128], P('row'), may hold values from -0.5 to 0.5
- group_start: int32 [4], replicated, may hold values from 0 to 192
- group_span: int32 [4], replicated, may hold values from 63 to 255
Outputs:
- panel_out: float32 [131072, 2048], P('row', 'col')
All inputs are finite; a program needn't handle non-finite values.
Results may differ from a plain program's by a relative error of at most 0.00011.
Values sent between devices are 32-bit elements; how exact they have to be, the bound alone decides.
A program may use at most 64 MiB of HBM per device.

v0:
```python
import jax
import jax.numpy as jnp
from jax import lax
from jax.sharding import PartitionSpec as P


def copy_for_each(value, axis):
    copies = jnp.broadcast_to(value, (lax.axis_size(axis), *value.shape))
    return lax.all_to_all(copies, axis, split_axis=0, concat_axis=0, tiled=True)


def laid_out(blocks, dim):
    blocks = jnp.moveaxis(blocks, 0, dim)
    lengths = blocks.shape
    return blocks.reshape(*lengths[:dim], lengths[dim] * lengths[dim + 1], *lengths[dim + 2 :])


def gathered_copies(value, axis, dim):
    blocks = copy_for_each(value, axis)
    return laid_out(blocks, dim)


def sent_together(arrays, axis, dim, along):
    ends, at = ([], 0)
    for a in arrays[:-1]:
        at += a.shape[along]
        ends.append(at)
    both = jnp.concatenate(arrays, axis=along)
    return tuple(jnp.split(gathered_copies(both, axis, dim), ends, axis=along))


def from_behind(value, axis, by):
    devices = lax.axis_size(axis)
    pairs = [(i, i + by) for i in range(devices) if 0 <= i + by < devices]
    return lax.ppermute(value, axis, pairs)


def project(vectors, band):
    return jnp.einsum("bk,bc->kc", vectors, band, precision=lax.Precision.HIGHEST)


def expand(vectors, factor, inner):
    scaled = jnp.dot(factor, inner, precision=lax.Precision.HIGHEST)
    return jnp.dot(vectors, scaled, precision=lax.Precision.HIGHEST)


def reflect(vectors, factor, band):
    return expand(vectors, factor, project(vectors, band))


def local(panel, inner_vecs, inner_factor, border_vecs, border_factor, group_start, group_span):
    width = inner_factor.shape[-1]
    height = panel.shape[0]
    steps = inner_factor.shape[1]
    index = lax.axis_index("row")
    whole_inner, whole_border = sent_together((inner_vecs, border_vecs), "col", 2, 0)
    whole_inner = whole_inner[0]
    whole_border = whole_border[0]
    fac_inner = inner_factor[0]
    fac_border = border_factor[0]
    lower_vecs, lower_factor = from_behind(
        (whole_border[0::2, width:, :], fac_border[0::2]), "row", 1
    )
    for step in range(steps):
        start = group_start[step]
        span = group_span[step]
        active = (index >= start) & (index < start + span)
        if step % 2 == 1:
            upper = panel[: 2 * width]
            panel = panel.at[: 2 * width].set(
                upper - reflect(whole_inner[step], fac_inner[step], upper)
            )
            lower = panel[2 * width :]
            change = reflect(whole_border[step], fac_border[step], lower)
            change = jnp.where(active, change, jnp.zeros_like(change))
            panel = panel.at[2 * width :].set(lower - change)
            continue
        middle = panel[width : 3 * width]
        panel = panel.at[width : 3 * width].set(
            middle - reflect(whole_inner[step], fac_inner[step], middle)
        )
        half_step = step // 2
        upper_vecs = whole_border[step][:width]
        upper_part = project(upper_vecs, panel[height - width :])
        lower_part = project(lower_vecs[half_step], panel[:width])
        from_below = from_behind(lower_part, "row", -1)
        from_above = from_behind(upper_part, "row", 1)
        previous = (index - 1 >= start) & (index - 1 < start + span)
        own_change = expand(upper_vecs, fac_border[step], upper_part + from_below)
        own_change = jnp.where(active, own_change, jnp.zeros_like(own_change))
        prior_change = expand(
            lower_vecs[half_step], lower_factor[half_step], from_above + lower_part
        )
        prior_change = jnp.where(previous, prior_change, jnp.zeros_like(prior_change))
        panel = panel.at[height - width :].set(panel[height - width :] - own_change)
        panel = panel.at[:width].set(panel[:width] - prior_change)
    return panel


def solution(mesh):
    placed = (
        P("row", "col"),
        P("row", None, "col", None),
        P("row", None, None, None),
        P("row", None, "col", None),
        P("row", None, None, None),
        P(),
        P(),
    )
    return jax.shard_map(
        local, mesh=mesh, in_specs=placed, out_specs=P("row", "col"), check_vma=False
    )
```

profile of v0, /device:TPU:32, one launch (start us, length us, event | category | flops | bytes accessed | tf_op | source)
XLA Modules:
  0.0 105.8 jit_solution(6932694675020516144)
XLA Ops:
  0.0 1.6 %copy.22 = f32[512,1024]{1,0:T(8,128)S(1)} copy(f32[512,1024]{1,0:T(8,128)} %param.27) | data formatting | bytes 4194304
  1.8 4.6 %all_to_all.5 = f32[2,2,4,128,128]{4,3,2,1,0:T(8,128)S(1)} all-to-all(f32[2,2,4,128,128]{4,3,2,1,0:T(8,128)S(1)} %broadcast_in_dim.3), channel_id=1, replica_groups=mesh['row'=256,'col'=2] {'col'}, dimensions={0} | all-to-all | bytes 2097152 | tf_op jit(solution)/shard_map/all_to_all | solution.py:9
  6.5 4.3 %collective-permute-start = (f32[2,128,128]{2,1,0:T(8,128)S(1)}, f32[2,128,128]{2,1,0:T(8,128)S(1)}, u32[]{:S(2)}, u32[]{:S(2)}) collective-permute-start(f32[2,128,128]{2,1,0:T(8,128)S(1)} %slice.344), channel_id=1, source_target_pairs={{0,2},{2,4},{4,6},{6,8},{8,10},{10,12},{12,14},{14,16},{16,18},{18... | collective-permute-start | bytes 393224 | tf_op jit(solution)/shard_map/ppermute | solution.py:35
  12.3 1.8 %fusion.56 = f32[1024,128]{1,0:T(8,128)S(1)} fusion(f32[128,1024]{1,0:T(8,128)S(1)} %fusion.26, f32[1,4,128,128]{3,2,1,0:T(8,128)} %param.29), kind=kOutput, calls=%fused_computation.74 | convolution fusion | flops 201326592 | bytes 1114112 | tf_op jit(solution)/shard_map/dot_general | solution.py:43
  14.2 1.3 %fusion.7 = f32[512,1024]{1,0:T(8,128)S(1)} fusion(f32[512,1024]{1,0:T(8,128)S(1)} %copy.22, f32[256,128]{1,0:T(8,128)S(1)} %bitcast.110, f32[1024,128]{1,0:T(8,128)S(1)} %fusion.56), kind=kOutput, calls=%fused_computation.13 | convolution fusion | flops 402915328 | bytes 2752512 | tf_op jit(solution)/shard_map/dot_general | solution.py:44
  15.5 1.4 %fusion.42 = f32[128,1024]{1,0:T(8,128)} fusion(f32[512,1024]{1,0:T(8,128)S(1)} %fusion.7, f32[2,4,2,128,128]{4,3,2,1,0:T(8,128)S(1)} %bitcast.95), kind=kOutput, calls=%fused_computation.54 | convolution fusion | flops 201326592 | bytes 1114112 | tf_op jit(solution)/shard_map/bk,bc->kc/dot_general | solution.py:39
  16.9 4.3 %collective-permute-start.2 = (f32[128,1024]{1,0:T(8,128)}, f32[128,1024]{1,0:T(8,128)}, u32[]{:S(2)}, u32[]{:S(2)}) collective-permute-start(f32[128,1024]{1,0:T(8,128)} %fusion.42), channel_id=1, source_target_pairs={{0,2},{2,4},{4,6},{6,8},{8,10},{10,12},{12,14},{14,16},{16,18},{18... | collective-permute-start | bytes 1572872 | tf_op jit(solution)/shard_map/ppermute | solution.py:35
  21.2 2.1 %collective-permute-done = f32[2,128,128]{2,1,0:T(8,128)S(1)} collective-permute-done((f32[2,128,128]{2,1,0:T(8,128)S(1)}, f32[2,128,128]{2,1,0:T(8,128)S(1)}, u32[]{:S(2)}, u32[]{:S(2)}) %collective-permute-start) | collective-permute-done | bytes 131104 | tf_op jit(solution)/shard_map/ppermute | solution.py:35
  23.4 1.4 %fusion.30 = f32[128,1024]{1,0:T(8,128)} fusion(f32[512,1024]{1,0:T(8,128)S(1)} %fusion.7, f32[2,128,128]{2,1,0:T(8,128)S(1)} %collective-permute-done), kind=kOutput, calls=%fused_computation.41 | convolution fusion | flops 201326592 | bytes 1114112 | tf_op jit(solution)/shard_map/bk,bc->kc/dot_general | solution.py:39
  24.8 6.2 %collective-permute-start.1 = (f32[128,1024]{1,0:T(8,128)}, f32[128,1024]{1,0:T(8,128)}, u32[]{:S(2)}, u32[]{:S(2)}) collective-permute-start(f32[128,1024]{1,0:T(8,128)} %fusion.30), channel_id=1, source_target_pairs={{2,0},{4,2},{6,4},{8,6},{10,8},{12,10},{14,12},{16,14},{18,16},{20... | collective-permute-start | bytes 1572872 | tf_op jit(solution)/shard_map/ppermute | solution.py:35
  31.6 2.1 %collective-permute-start.3 = (f32[2,128,128]{2,1,0:T(8,128)}, f32[2,128,128]{2,1,0:T(8,128)}, u32[]{:S(2)}, u32[]{:S(2)}) collective-permute-start(f32[2,128,128]{2,1,0:T(8,128)} %slice.349), channel_id=1, source_target_pairs={{0,2},{2,4},{4,6},{6,8},{8,10},{10,12},{12,14},{14,16},{16,18},{18... | collective-permute-start | bytes 393224 | tf_op jit(solution)/shard_map/ppermute | solution.py:35
  39.4 5.1 %collective-permute-done.3 = f32[2,128,128]{2,1,0:T(8,128)} collective-permute-done((f32[2,128,128]{2,1,0:T(8,128)}, f32[2,128,128]{2,1,0:T(8,128)}, u32[]{:S(2)}, u32[]{:S(2)}) %collective-permute-start.3) | collective-permute-done | bytes 131104 | tf_op jit(solution)/shard_map/ppermute | solution.py:35
  44.5 2.2 %fusion.36 = f32[1024,128]{1,0:T(8,128)S(1)} fusion(f32[128,1024]{1,0:T(8,128)} %collective-permute-done.2, f32[128,1024]{1,0:T(8,128)} %fusion.30, f32[2,128,128]{2,1,0:T(8,128)} %collective-permute-done.3), kind=kOutput, calls=%fused_computation.48 | convolution fusion | flops 201457664 | bytes 1638400 | tf_op jit(solution)/shard_map/dot_general | solution.py:43
  46.8 2.2 %fusion.38 = f32[1024,128]{1,0:T(8,128)S(1)} fusion(f32[128,1024]{1,0:T(8,128)} %fusion.42, f32[128,1024]{1,0:T(8,128)} %collective-permute-done.1, f32[1,4,128,128]{3,2,1,0:T(8,128)} %param.31), kind=kOutput, calls=%fused_computation.50 | convolution fusion | flops 201457664 | bytes 1638400 | tf_op jit(solution)/shard_map/dot_general | solution.py:43
  51.3 1.0 fusion.53
  52.3 1.3 %fusion.6 = f32[512,1024]{1,0:T(8,128)S(1)} fusion(f32[512,1024]{1,0:T(8,128)S(1)} %fusion.13, f32[256,128]{1,0:T(8,128)S(1)} %bitcast.108, f32[1024,128]{1,0:T(8,128)S(1)} %fusion.53), kind=kOutput, calls=%fused_computation.11 | convolution fusion | flops 402915328 | bytes 2752512 | tf_op jit(solution)/shard_map/dot_general | solution.py:44
  54.4 1.9 %fusion.51 = f32[1024,128]{1,0:T(8,128)S(1)} fusion(f32[128,1024]{1,0:T(8,128)S(1)} %fusion.22, f32[1,4,128,128]{3,2,1,0:T(8,128)} %param.31), kind=kOutput, calls=%fused_computation.69 | convolution fusion | flops 201326592 | bytes 1114112 | tf_op jit(solution)/shard_map/dot_general | solution.py:43
  56.3 1.4 %fusion.1 = f32[512,1024]{1,0:T(8,128)S(1)} fusion(f32[512,1024]{1,0:T(8,128)S(1)} %fusion.6, f32[256,128]{1,0:T(8,128)S(1)} %bitcast.102, f32[1024,128]{1,0:T(8,128)S(1)} %fusion.51, pred[]{:T(512)S(6)} %and.51), kind=kOutput, calls=%fused_computation.3 | convolution fusion | flops 403177472 | bytes 2752513 | tf_op jit(solution)/shard_map/dot_general | solution.py:44
  58.4 1.0 fusion.49
  59.4 1.6 %fusion.5 = f32[512,1024]{1,0:T(8,128)S(1)} fusion(f32[512,1024]{1,0:T(8,128)S(1)} %fusion.1, f32[256,128]{1,0:T(8,128)S(1)} %bitcast.106, f32[1024,128]{1,0:T(8,128)S(1)} %fusion.49), kind=kOutput, calls=%fused_computation.9 | convolution fusion | flops 402915328 | bytes 2752512 | tf_op jit(solution)/shard_map/dot_general | solution.py:44
  60.9 1.4 %fusion.28 = f32[128,1024]{1,0:T(8,128)} fusion(f32[512,1024]{1,0:T(8,128)S(1)} %fusion.5, f32[2,128,128]{2,1,0:T(8,128)S(1)} %copy-done.5), kind=kOutput, calls=%fused_computation.39 | convolution fusion | flops 201326592 | bytes 1114112 | tf_op jit(solution)/shard_map/bk,bc->kc/dot_general | solution.py:39
  62.4 5.8 %collective-permute-start.4 = (f32[128,1024]{1,0:T(8,128)}, f32[128,1024]{1,0:T(8,128)}, u32[]{:S(2)}, u32[]{:S(2)}) collective-permute-start(f32[128,1024]{1,0:T(8,128)} %fusion.28), channel_id=1, source_target_pairs={{2,0},{4,2},{6,4},{8,6},{10,8},{12,10},{14,12},{16,14},{18,16},{20... | collective-permute-start | bytes 1572872 | tf_op jit(solution)/shard_map/ppermute | solution.py:35
  73.0 2.1 %collective-permute-start.5 = (f32[128,1024]{1,0:T(8,128)S(1)}, f32[128,1024]{1,0:T(8,128)S(1)}, u32[]{:S(2)}, u32[]{:S(2)}) collective-permute-start(f32[128,1024]{1,0:T(8,128)S(1)} %fusion.40), channel_id=1, source_target_pairs={{0,2},{2,4},{4,6},{6,8},{8,10},{10,12},{12,14},{14,16},{16,18},{18... | collective-permute-start | bytes 1572872 | tf_op jit(solution)/shard_map/ppermute | solution.py:35
  75.1 4.0 %collective-permute-done.4 = f32[128,1024]{1,0:T(8,128)} collective-permute-done((f32[128,1024]{1,0:T(8,128)}, f32[128,1024]{1,0:T(8,128)}, u32[]{:S(2)}, u32[]{:S(2)}) %collective-permute-start.4) | collective-permute-done | bytes 524320 | tf_op jit(solution)/shard_map/ppermute | solution.py:35
  79.1 2.0 %fusion.34 = f32[1024,128]{1,0:T(8,128)S(1)} fusion(f32[128,1024]{1,0:T(8,128)S(1)} %fusion.40, f32[128,1024]{1,0:T(8,128)} %collective-permute-done.4, f32[1,4,128,128]{3,2,1,0:T(8,128)} %param.31), kind=kOutput, calls=%fused_computation.46 | convolution fusion | flops 201457664 | bytes 1638400 | tf_op jit(solution)/shard_map/dot_general | solution.py:43
  81.9 11.4 %collective-permute-done.5 = f32[128,1024]{1,0:T(8,128)S(1)} collective-permute-done((f32[128,1024]{1,0:T(8,128)S(1)}, f32[128,1024]{1,0:T(8,128)S(1)}, u32[]{:S(2)}, u32[]{:S(2)}) %collective-permute-start.5) | collective-permute-done | bytes 524320 | tf_op jit(solution)/shard_map/ppermute | solution.py:35
  93.3 2.0 %fusion.32 = f32[1024,128]{1,0:T(8,128)S(1)} fusion(f32[128,1024]{1,0:T(8,128)S(1)} %collective-permute-done.5, f32[128,1024]{1,0:T(8,128)} %fusion.28, f32[2,128,128]{2,1,0:T(8,128)} %collective-permute-done.3), kind=kOutput, calls=%fused_computation.44 | convolution fusion | flops 201457664 | bytes 1638400 | tf_op jit(solution)/shard_map/dot_general | solution.py:43
  95.4 0.8 fusion.9
  96.9 1.8 %fusion.46 = f32[1024,128]{1,0:T(8,128)S(1)} fusion(f32[128,1024]{1,0:T(8,128)S(1)} %fusion.18, f32[1,4,128,128]{3,2,1,0:T(8,128)} %param.29), kind=kOutput, calls=%fused_computation.64 | convolution fusion | flops 201326592 | bytes 1114112 | tf_op jit(solution)/shard_map/dot_general | solution.py:43
  98.7 1.3 %fusion.4 = f32[512,1024]{1,0:T(8,128)S(1)} fusion(f32[512,1024]{1,0:T(8,128)S(1)} %fusion.9, f32[256,128]{1,0:T(8,128)S(1)} %bitcast.104, f32[1024,128]{1,0:T(8,128)S(1)} %fusion.46), kind=kOutput, calls=%fused_computation.7 | convolution fusion | flops 402915328 | bytes 2752512 | tf_op jit(solution)/shard_map/dot_general | solution.py:44
  100.8 1.8 %fusion.44 = f32[1024,128]{1,0:T(8,128)S(1)} fusion(f32[128,1024]{1,0:T(8,128)S(1)} %fusion.16, f32[1,4,128,128]{3,2,1,0:T(8,128)} %param.31), kind=kOutput, calls=%fused_computation.62 | convolution fusion | flops 201326592 | bytes 1114112 | tf_op jit(solution)/shard_map/dot_general | solution.py:43
  102.6 3.2 %fusion.3 = f32[512,1024]{1,0:T(8,128)} fusion(f32[512,1024]{1,0:T(8,128)} %copy-done, f32[256,128]{1,0:T(8,128)S(1)} %bitcast.100, f32[1024,128]{1,0:T(8,128)S(1)} %fusion.44, pred[]{:T(512)S(6)} %and.54), kind=kOutput, calls=%fused_computation.5 | convolution fusion | flops 403177472 | bytes 2752513 | tf_op jit(solution)/shard_map/dot_general | solution.py:44
  (45 shorter events, 10.3 us)
Async XLA Ops:
  0.0 1.7 %copy-start.9 = (f32[1,4,128,128]{3,2,1,0:T(8,128)S(1)}, f32[1,4,128,128]{3,2,1,0:T(8,128)}, u32[]{:S(2)}) copy-start(f32[1,4,128,128]{3,2,1,0:T(8,128)} %param.28) | copy-start | bytes 786436
  0.0 1.7 %copy-start.8 = (f32[1,4,128,128]{3,2,1,0:T(8,128)S(1)}, f32[1,4,128,128]{3,2,1,0:T(8,128)}, u32[]{:S(2)}) copy-start(f32[1,4,128,128]{3,2,1,0:T(8,128)} %param.30) | copy-start | bytes 786436
  6.5 16.8 %collective-permute-start = (f32[2,128,128]{2,1,0:T(8,128)S(1)}, f32[2,128,128]{2,1,0:T(8,128)S(1)}, u32[]{:S(2)}, u32[]{:S(2)}) collective-permute-start(f32[2,128,128]{2,1,0:T(8,128)S(1)} %slice.344), channel_id=1, source_target_pairs={{0,2},{2,4},{4,6},{6,8},{8,10},{10,12},{12,14},{14,16},{16,18},{18... | collective-permute-start | bytes 393224 | tf_op jit(solution)/shard_map/ppermute | solution.py:35
  14.2 16.8 %copy-start.3 = (f32[1,4,128,128]{3,2,1,0:T(8,128)S(1)}, f32[1,4,128,128]{3,2,1,0:T(8,128)}, u32[]{:S(2)}) copy-start(f32[1,4,128,128]{3,2,1,0:T(8,128)} %param.31) | copy-start | bytes 786436
  14.2 19.6 %copy-start.10 = (s32[4]{0:T(128)S(1)}, s32[4]{0:T(128)}, u32[]{:S(2)}) copy-start(s32[4]{0:T(128)} %param.32) | copy-start | bytes 52
  14.2 21.4 %copy-start.11 = (s32[4]{0:T(128)S(1)}, s32[4]{0:T(128)}, u32[]{:S(2)}) copy-start(s32[4]{0:T(128)} %param.33) | copy-start | bytes 52
  16.9 27.6 %collective-permute-start.2 = (f32[128,1024]{1,0:T(8,128)}, f32[128,1024]{1,0:T(8,128)}, u32[]{:S(2)}, u32[]{:S(2)}) collective-permute-start(f32[128,1024]{1,0:T(8,128)} %fusion.42), channel_id=1, source_target_pairs={{0,2},{2,4},{4,6},{6,8},{8,10},{10,12},{12,14},{14,16},{16,18},{18... | collective-permute-start | bytes 1572872 | tf_op jit(solution)/shard_map/ppermute | solution.py:35
  23.4 8.3 %copy-start.4 = (f32[2,128,128]{2,1,0:T(8,128)}, f32[2,128,128]{2,1,0:T(8,128)S(1)}, u32[]{:S(2)}) copy-start(f32[2,128,128]{2,1,0:T(8,128)S(1)} %collective-permute-done) | copy-start | bytes 393220
  24.8 22.0 %collective-permute-start.1 = (f32[128,1024]{1,0:T(8,128)}, f32[128,1024]{1,0:T(8,128)}, u32[]{:S(2)}, u32[]{:S(2)}) collective-permute-start(f32[128,1024]{1,0:T(8,128)} %fusion.30), channel_id=1, source_target_pairs={{2,0},{4,2},{6,4},{8,6},{10,8},{12,10},{14,12},{16,14},{18,16},{20... | collective-permute-start | bytes 1572872 | tf_op jit(solution)/shard_map/ppermute | solution.py:35
  31.6 12.9 %collective-permute-start.3 = (f32[2,128,128]{2,1,0:T(8,128)}, f32[2,128,128]{2,1,0:T(8,128)}, u32[]{:S(2)}, u32[]{:S(2)}) collective-permute-start(f32[2,128,128]{2,1,0:T(8,128)} %slice.349), channel_id=1, source_target_pairs={{0,2},{2,4},{4,6},{6,8},{8,10},{10,12},{12,14},{14,16},{16,18},{18... | collective-permute-start | bytes 393224 | tf_op jit(solution)/shard_map/ppermute | solution.py:35
  39.4 10.4 %copy-start.5 = (f32[2,128,128]{2,1,0:T(8,128)S(1)}, f32[2,128,128]{2,1,0:T(8,128)}, u32[]{:S(2)}) copy-start(f32[2,128,128]{2,1,0:T(8,128)} %copy-done.4) | copy-start | bytes 393220
  46.7 3.8 %copy-start.2 = (f32[1,1,2,128,128]{4,3,2,1,0:T(8,128)S(1)}, f32[1,1,2,128,128]{4,3,2,1,0:T(8,128)}, u32[]{:S(2)}) copy-start(f32[1,1,2,128,128]{4,3,2,1,0:T(8,128)} %get-tuple-element.129) | copy-start | bytes 393220
  49.0 2.3 %copy-start.7 = (f32[1,4,128,128]{3,2,1,0:T(8,128)S(1)}, f32[1,4,128,128]{3,2,1,0:T(8,128)}, u32[]{:S(2)}) copy-start(f32[1,4,128,128]{3,2,1,0:T(8,128)} %param.29) | copy-start | bytes 786436
  54.4 3.3 %copy-start.1 = (f32[1,1,2,128,128]{4,3,2,1,0:T(8,128)S(1)}, f32[1,1,2,128,128]{4,3,2,1,0:T(8,128)}, u32[]{:S(2)}) copy-start(f32[1,1,2,128,128]{4,3,2,1,0:T(8,128)} %get-tuple-element.127) | copy-start | bytes 393220
  62.4 16.7 %collective-permute-start.4 = (f32[128,1024]{1,0:T(8,128)}, f32[128,1024]{1,0:T(8,128)}, u32[]{:S(2)}, u32[]{:S(2)}) collective-permute-start(f32[128,1024]{1,0:T(8,128)} %fusion.28), channel_id=1, source_target_pairs={{2,0},{4,2},{6,4},{8,6},{10,8},{12,10},{14,12},{16,14},{18,16},{20... | collective-permute-start | bytes 1572872 | tf_op jit(solution)/shard_map/ppermute | solution.py:35
  73.0 22.3 %copy-start.6 = (f32[2,128,128]{2,1,0:T(8,128)S(1)}, f32[2,128,128]{2,1,0:T(8,128)}, u32[]{:S(2)}) copy-start(f32[2,128,128]{2,1,0:T(8,128)} %copy-done.4) | copy-start | bytes 393220
  73.0 20.3 %collective-permute-start.5 = (f32[128,1024]{1,0:T(8,128)S(1)}, f32[128,1024]{1,0:T(8,128)S(1)}, u32[]{:S(2)}, u32[]{:S(2)}) collective-permute-start(f32[128,1024]{1,0:T(8,128)S(1)} %fusion.40), channel_id=1, source_target_pairs={{0,2},{2,4},{4,6},{6,8},{8,10},{10,12},{12,14},{14,16},{16,18},{18... | collective-permute-start | bytes 1572872 | tf_op jit(solution)/shard_map/ppermute | solution.py:35
  100.1 2.6 %copy-start = (f32[512,1024]{1,0:T(8,128)}, f32[512,1024]{1,0:T(8,128)S(1)}, u32[]{:S(2)}) copy-start(f32[512,1024]{1,0:T(8,128)S(1)} %fusion.4) | copy-start | bytes 6291460
where the time goes:
time: 107 us; the launch traced here: 106 us
  matrix products  40.2 us (38%)
  starting transfers between devices  24.6 us (23%)
  waiting for transfers between devices  22.6 us (21%)
  between operations  9.06 us (8%)
  local copies, waits for them, and re-layouts  4.69 us (4%)
  blocking collectives  4.58 us (4%)
    ppermute x6, starting transfers between devices, from_behind(): return lax.ppermute(value, axis, pairs)  24.6 us
    ppermute x6, waiting for transfers between devices, from_behind(): return lax.ppermute(value, axis, pairs)  22.6 us
    dot_general x10, matrix products, expand(): scaled = jnp.dot(factor, inner, precision=lax.Precision.HIGHEST)  17.9 us
    dot_general x10, matrix products, expand(): return jnp.dot(vectors, scaled, precision=lax.Precision.HIGHEST)  13.2 us
    dot_general x10, matrix products, project(): jnp.einsum('bk,bc->kc', vectors, band, precision=lax.Precision.HIGHEST)  9.18 us
    all_to_all x1, blocking collectives, copy_for_each(): return lax.all_to_all(copies, axis, split_axis=0, concat_axis=0, tiled=True)  4.58 us
  transfers between devices with their start and end apart: 6, of which 4 were waited for; matrix products, arithmetic and copies ran while one was open for 14% of the time, Pallas kernels for 0%

commit v1 on v0

v1 whole, which is shorter than its diff:
```python
import functools

import jax
import jax.numpy as jnp
from jax import lax
from jax.experimental import pallas as pl
from jax.experimental.pallas import tpu as pltpu
from jax.sharding import PartitionSpec as P

MESH = pl.DeviceIdType.MESH
F32 = jnp.float32
BF16 = jnp.bfloat16
CHUNKS = 4


def halves(value):
    high = value.astype(BF16)
    low = (value - high.astype(F32)).astype(BF16)
    return high, low


def product(a, b, dims=((1,), (0,))):
    def dot(left, right):
        return lax.dot_general(left, right, (dims, ((), ())), preferred_element_type=F32)

    return dot(a[0], b[0]) + (dot(a[0], b[1]) + dot(a[1], b[0]))


def kernel(
    rows,
    panel,
    inner_vecs,
    inner_factor,
    border_vecs,
    border_factor,
    group_start,
    group_span,
    out,
    state,
    vec_inner,
    vec_border,
    fac_inner,
    fac_border,
    q_high,
    q_low,
    lower_send,
    lower_all,
    corner_send,
    corner_all,
    above_first,
    below_first,
    above_second,
    below_second,
    share,
    raise_buf,
    load_sem,
    send_sem,
    recv_sem,
):
    row = lax.axis_index("row")
    col = lax.axis_index("col")
    height, width = panel.shape
    nb = height // 4
    chunk = width // CHUNKS
    half = nb // 2
    down = (lax.rem(row + 1, rows), col)
    up = (lax.rem(row + rows - 1, rows), col)
    mate = (row, 1 - col)
    mine = pl.ds(pl.multiple_of(col * nb, nb), nb)
    mine_half = pl.ds(pl.multiple_of(col * half, half), half)

    loads = []

    def load(src, dst):
        copy = pltpu.make_async_copy(src, dst, load_sem.at[len(loads)])
        copy.start()
        loads.append(copy)
        return copy

    load_border = [load(border_vecs.at[0, s], vec_border.at[s, mine]) for s in (0, 2, 1, 3)]
    load_fac_border = load(border_factor.at[0], fac_border)
    load_inner = load(inner_vecs.at[0], vec_inner.at[:, mine])
    load_fac_inner = load(inner_factor.at[0], fac_inner)
    load_panel = [
        load(panel.at[:, pl.ds(k * chunk, chunk)], state.at[k]) for k in range(CHUNKS)
    ]

    barrier = pltpu.get_barrier_semaphore()
    for peer in (down, up, mate):
        pl.semaphore_signal(barrier, inc=1, device_id=peer, device_id_type=MESH)
    pl.semaphore_wait(barrier, 3)

    sends = []

    def send(src, dst, peer):
        at = len(sends)
        copy = pltpu.make_async_remote_copy(
            src_ref=src,
            dst_ref=dst,
            send_sem=send_sem.at[at],
            recv_sem=recv_sem.at[at],
            device_id=peer,
            device_id_type=MESH,
        )
        copy.start()
        sends.append(copy)
        return copy

    def send_down_first(k):
        return send(
            panel.at[pl.ds(3 * nb, nb), pl.ds(k * chunk, chunk)], above_first.at[k], down
        )

    vec_from_mate = {}
    vec_from_mate[0] = send(border_vecs.at[0, 0], vec_border.at[0, mine], mate)
    down_first = [send_down_first(0)]
    up_first = [
        send(panel.at[pl.ds(0, nb), pl.ds(k * chunk, chunk)], below_first.at[k], up)
        for k in range(CHUNKS)
    ]
    vec_from_mate[2] = send(border_vecs.at[0, 2], vec_border.at[2, mine], mate)
    down_first.append(send_down_first(1))
    inner_from_mate = send(inner_vecs.at[0], vec_inner.at[:, mine], mate)
    vec_from_mate[1] = send(border_vecs.at[0, 1], vec_border.at[1, mine], mate)
    vec_from_mate[3] = send(border_vecs.at[0, 3], vec_border.at[3, mine], mate)

    def build(slot, vectors, factor, scale):
        v = halves(vectors)
        w = halves(product(v, halves(factor)))
        q = product(w, v, ((1,), (1,)))
        if scale is not None:
            q = q * scale
        high, low = halves(q)
        q_high[slot] = high
        q_low[slot] = low
        return q

    def active(s):
        start = group_start[s]
        span = group_span[s]
        return ((row >= start) & (row < start + span)).astype(F32)

    def build_border(s):
        return build(4 + s, vec_border[s], fac_border[s], active(s))

    for copy in load_border:
        copy.wait()
    load_fac_border.wait()

    vec_from_mate[0].wait_recv()
    q = build_border(0)
    lower_send[...] = q[nb:]
    vec_from_mate[2].wait_recv()
    q = build_border(2)
    corner_send[...] = q[nb:, nb:]
    lower_down = send(lower_send.at[mine_half], lower_all.at[mine_half], down)
    corner_down = send(corner_send.at[mine_half], corner_all.at[mine_half], down)
    for k in range(2, CHUNKS):
        down_first.append(send_down_first(k))

    load_inner.wait()
    load_fac_inner.wait()
    inner_from_mate.wait_recv()
    vec_from_mate[1].wait_recv()
    vec_from_mate[3].wait_recv()
    for slot in (0, 1, 2, 3):
        build(slot, vec_inner[slot], fac_inner[slot], None)
        if slot % 2 == 1:
            build_border(slot)

    def q_of(slot, r=slice(None), c=slice(None)):
        return q_high[slot, r, c], q_low[slot, r, c]

    def apply(slot, band):
        return band - product(q_of(slot), halves(band))

    up_second, down_second = [], []

    def lower_side(k):
        if k == 0:
            load_panel_wait(0)
        else:
            load_panel_wait(k)
        state[k, nb : 3 * nb] = apply(0, state[k, nb : 3 * nb])
        up_first[k].wait_recv()
        last = state[k, 3 * nb :]
        band = jnp.concatenate([last, below_first[k]], axis=0)
        last = last - product(q_of(4, slice(0, nb)), halves(band))
        band = jnp.concatenate([state[k, 2 * nb : 3 * nb], last], axis=0)
        band = apply(5, band)
        state[k, 2 * nb :] = band
        share[k] = product(q_of(6, slice(nb, None), slice(0, nb)), halves(band[nb:]))

    def load_panel_wait(k):
        load_panel[k].wait()

    def send_share(k):
        down_second.append(send(share.at[k], above_second.at[k], down))

    def upper_side(k):
        down_first[k].wait_recv()
        first = state[k, :nb]
        band = jnp.concatenate([above_first[k], first], axis=0)
        first = first - product(halves(lower_all[...]), halves(band))
        band = jnp.concatenate([first, state[k, nb : 2 * nb]], axis=0)
        band = apply(1, band)
        state[k, : 2 * nb] = band
        raise_buf[k] = band[:nb]

    def send_raise(k):
        up_second.append(send(raise_buf.at[k], below_second.at[k], up))

    def middle(k):
        state[k, nb : 3 * nb] = apply(2, state[k, nb : 3 * nb])

    def finish(k):
        down_second[k].wait_recv()
        first = state[k, :nb]
        first = first - (product(halves(corner_all[...]), halves(first)) + above_second[k])
        band = jnp.concatenate([first, state[k, nb : 2 * nb]], axis=0)
        out[: 2 * nb, k * chunk : (k + 1) * chunk] = apply(3, band)
        up_second[k].wait_recv()
        last = state[k, 3 * nb :]
        band = jnp.concatenate([last, below_second[k]], axis=0)
        last = last - product(q_of(6, slice(0, nb)), halves(band))
        band = jnp.concatenate([state[k, 2 * nb : 3 * nb], last], axis=0)
        out[2 * nb :, k * chunk : (k + 1) * chunk] = apply(7, band)

    lower_side(0)
    lower_side(1)
    send_share(0)
    lower_down.wait_recv()
    corner_down.wait_recv()
    lower_pair = send(lower_all.at[mine_half], lower_all.at[mine_half], mate)
    corner_pair = send(corner_all.at[mine_half], corner_all.at[mine_half], mate)
    lower_pair.wait_recv()
    corner_pair.wait_recv()
    upper_side(0)
    send_share(1)
    upper_side(1)
    send_raise(0)
    lower_side(2)
    send_raise(1)
    upper_side(2)
    send_share(2)
    lower_side(3)
    send_raise(2)
    upper_side(3)
    send_share(3)
    middle(0)
    send_raise(3)
    for k in range(1, CHUNKS):
        middle(k)
    for k in range(CHUNKS):
        finish(k)
    for copy in sends:
        copy.wait_send()


def local(panel, inner_vecs, inner_factor, border_vecs, border_factor, group_start, group_span, *, rows):
    height, width = panel.shape
    nb = height // 4
    chunk = width // CHUNKS
    steps = inner_factor.shape[1]
    vmem, dma = pltpu.VMEM, pltpu.SemaphoreType.DMA
    anywhere = pl.BlockSpec(memory_space=pl.ANY)
    scalars = pl.BlockSpec(memory_space=pltpu.SMEM)
    copies = 4 * CHUNKS + 5 + 4
    return pl.pallas_call(
        functools.partial(kernel, rows),
        out_shape=jax.ShapeDtypeStruct(panel.shape, F32),
        in_specs=[anywhere] * 5 + [scalars] * 2,
        out_specs=pl.BlockSpec(memory_space=pltpu.VMEM),
        scratch_shapes=[
            vmem((CHUNKS, height, chunk), F32),
            vmem((steps, 2 * nb, nb), F32),
            vmem((steps, 2 * nb, nb), F32),
            vmem((steps, nb, nb), F32),
            vmem((steps, nb, nb), F32),
            vmem((2 * steps, 2 * nb, 2 * nb), BF16),
            vmem((2 * steps, 2 * nb, 2 * nb), BF16),
            vmem((nb, 2 * nb), F32),
            vmem((nb, 2 * nb), F32),
            vmem((nb, nb), F32),
            vmem((nb, nb), F32),
            vmem((CHUNKS, nb, chunk), F32),
            vmem((CHUNKS, nb, chunk), F32),
            vmem((CHUNKS, nb, chunk), F32),
            vmem((CHUNKS, nb, chunk), F32),
            vmem((CHUNKS, nb, chunk), F32),
            vmem((CHUNKS, nb, chunk), F32),
            dma((7 + CHUNKS,)),
            dma((copies,)),
            dma((copies,)),
        ],
        compiler_params=pltpu.CompilerParams(
            collective_id=0, has_side_effects=True, vmem_limit_bytes=48 * 2**20
        ),
        name="diamonds",
    )(panel, inner_vecs, inner_factor, border_vecs, border_factor, group_start, group_span)


def solution(mesh):
    placed = (
        P("row", "col"),
        P("row", None, "col", None),
        P("row", None, None, None),
        P("row", None, "col", None),
        P("row", None, None, None),
        P(),
        P(),
    )
    return jax.shard_map(
        functools.partial(local, rows=mesh.shape["row"]),
        mesh=mesh,
        in_specs=placed,
        out_specs=P("row", "col"),
        check_vma=False,
    )
```

time: 107 us -> 53.8 us (0.50)
  the two profiles are of different devices: /device:TPU:32 before, /device:TPU:1 now
where the time goes in v1:
time: 53.8 us; the launch traced here: 53.5 us
  Pallas kernels  45.5 us (85%)
  local copies, waits for them, and re-layouts  8.02 us (15%)
    pallas_call x1, Pallas kernels, local(): pl.pallas_call(functools.partial(kernel, rows), out_shape=jax.ShapeDtypeS...  45.5 us
    unnamed x15, local copies, waits for them, and re-layouts  8.02 us

profile of v1, /device:TPU:1, one launch (start us, length us, event | category | flops | bytes accessed | tf_op | source)
XLA Modules:
  0.0 53.5 jit_solution(9353072996834388383)
XLA Ops:
  0.0 0.0 copy-start
  0.0 1.6 %copy-done = f32[512,1024]{1,0:T(8,128)S(1)} copy-done((f32[512,1024]{1,0:T(8,128)S(1)}, f32[512,1024]{1,0:T(8,128)}, u32[]{:S(2)}) %copy-start) | copy-done | bytes 2097176
  1.6 0.0 copy-start.1
  1.6 0.9 %copy-done.1 = f32[1,4,128,128]{3,2,1,0:T(8,128)S(1)} copy-done((f32[1,4,128,128]{3,2,1,0:T(8,128)S(1)}, f32[1,4,128,128]{3,2,1,0:T(8,128)}, u32[]{:S(2)}) %copy-start.1) | copy-done | bytes 262168
  2.5 0.0 copy-start.2
  2.5 0.9 %copy-done.2 = f32[1,4,128,128]{3,2,1,0:T(8,128)S(1)} copy-done((f32[1,4,128,128]{3,2,1,0:T(8,128)S(1)}, f32[1,4,128,128]{3,2,1,0:T(8,128)}, u32[]{:S(2)}) %copy-start.2) | copy-done | bytes 262168
  3.5 0.0 copy-start.3
  3.5 0.9 %copy-done.3 = f32[1,4,128,128]{3,2,1,0:T(8,128)S(1)} copy-done((f32[1,4,128,128]{3,2,1,0:T(8,128)S(1)}, f32[1,4,128,128]{3,2,1,0:T(8,128)}, u32[]{:S(2)}) %copy-start.3) | copy-done | bytes 262168
  4.4 0.0 copy-start.4
  4.4 0.9 %copy-done.4 = f32[1,4,128,128]{3,2,1,0:T(8,128)S(1)} copy-done((f32[1,4,128,128]{3,2,1,0:T(8,128)S(1)}, f32[1,4,128,128]{3,2,1,0:T(8,128)}, u32[]{:S(2)}) %copy-start.4) | copy-done | bytes 262168
  5.4 0.0 copy-start.5
  5.4 0.7 %copy-done.5 = s32[4]{0:T(128)S(1)} copy-done((s32[4]{0:T(128)S(1)}, s32[4]{0:T(128)}, u32[]{:S(2)}) %copy-start.5) | copy-done | bytes 40
  6.0 0.0 copy-start.6
  6.1 0.7 %copy-done.6 = s32[4]{0:T(128)S(1)} copy-done((s32[4]{0:T(128)S(1)}, s32[4]{0:T(128)}, u32[]{:S(2)}) %copy-start.6) | copy-done | bytes 40
  6.7 45.5 %diamonds.1 = f32[512,1024]{1,0:T(8,128)S(1)} custom-call(f32[512,1024]{1,0:T(8,128)S(1)} %copy-done, f32[1,4,128,128]{3,2,1,0:T(8,128)S(1)} %copy-done.1, f32[1,4,128,128]{3,2,1,0:T(8,128)S(1)} %copy-done.2, f32[1,4,128,128]{3,2,1,0:T(8,128)S(1)} %copy-done.3, f32[1,4,128,128]{3,2,1,0:T(8,128)S(1)} %copy-done.4, s32[4]{0:T(128)S(1)} %copy-done.5, ...), custom_call_target="tpu_custom_call" | custom-call | tf_op jit(solution)/shard_map/diamonds/pallas_call | solution.py:269
  52.2 1.3 %copy.9 = f32[512,1024]{1,0:T(8,128)} copy(f32[512,1024]{1,0:T(8,128)S(1)} %diamonds.1) | data formatting | bytes 4194304
Async XLA Ops:
  0.0 1.6 %copy-start = (f32[512,1024]{1,0:T(8,128)S(1)}, f32[512,1024]{1,0:T(8,128)}, u32[]{:S(2)}) copy-start(f32[512,1024]{1,0:T(8,128)} %panel.1) | copy-start | bytes 6291460
  1.6 0.9 %copy-start.1 = (f32[1,4,128,128]{3,2,1,0:T(8,128)S(1)}, f32[1,4,128,128]{3,2,1,0:T(8,128)}, u32[]{:S(2)}) copy-start(f32[1,4,128,128]{3,2,1,0:T(8,128)} %inner_vecs.1) | copy-start | bytes 786436
  2.5 0.9 %copy-start.2 = (f32[1,4,128,128]{3,2,1,0:T(8,128)S(1)}, f32[1,4,128,128]{3,2,1,0:T(8,128)}, u32[]{:S(2)}) copy-start(f32[1,4,128,128]{3,2,1,0:T(8,128)} %inner_factor.1) | copy-start | bytes 786436
  3.5 0.9 %copy-start.3 = (f32[1,4,128,128]{3,2,1,0:T(8,128)S(1)}, f32[1,4,128,128]{3,2,1,0:T(8,128)}, u32[]{:S(2)}) copy-start(f32[1,4,128,128]{3,2,1,0:T(8,128)} %border_vecs.1) | copy-start | bytes 786436
  4.4 0.9 %copy-start.4 = (f32[1,4,128,128]{3,2,1,0:T(8,128)S(1)}, f32[1,4,128,128]{3,2,1,0:T(8,128)}, u32[]{:S(2)}) copy-start(f32[1,4,128,128]{3,2,1,0:T(8,128)} %border_factor.1) | copy-start | bytes 786436
  5.4 0.7 %copy-start.5 = (s32[4]{0:T(128)S(1)}, s32[4]{0:T(128)}, u32[]{:S(2)}) copy-start(s32[4]{0:T(128)} %group_start.1) | copy-start | bytes 52
  6.0 0.7 %copy-start.6 = (s32[4]{0:T(128)S(1)}, s32[4]{0:T(128)}, u32[]{:S(2)}) copy-start(s32[4]{0:T(128)} %group_span.1) | copy-start | bytes 52

commit v2 on v1

--- a/solution.py
+++ b/solution.py
@@ -53,6 +53,8 @@
     below_second,
     share,
     raise_buf,
+    start_ref,
+    span_ref,
     load_sem,
     send_sem,
     recv_sem,
@@ -63,8 +65,9 @@
     nb = height // 4
     chunk = width // CHUNKS
     half = nb // 2
-    down = (lax.rem(row + 1, rows), col)
-    up = (lax.rem(row + rows - 1, rows), col)
+    has_up, has_down = row > 0, row < rows - 1
+    down = (jnp.minimum(row + 1, rows - 1), col)
+    up = (jnp.maximum(row - 1, 0), col)
     mate = (row, 1 - col)
     mine = pl.ds(pl.multiple_of(col * nb, nb), nb)
     mine_half = pl.ds(pl.multiple_of(col * half, half), half)
@@ -85,44 +88,85 @@
         load(panel.at[:, pl.ds(k * chunk, chunk)], state.at[k]) for k in range(CHUNKS)
     ]
 
+    load_start = load(group_start, start_ref)
+    load_span = load(group_span, span_ref)
+
     barrier = pltpu.get_barrier_semaphore()
-    for peer in (down, up, mate):
+
+    def greet(peer):
         pl.semaphore_signal(barrier, inc=1, device_id=peer, device_id_type=MESH)
-    pl.semaphore_wait(barrier, 3)
+
+    pl.when(has_up)(lambda: greet(up))
+    pl.when(has_down)(lambda: greet(down))
+    greet(mate)
+
+    @pl.when(jnp.logical_not(has_up))
+    def _():
+        lower_all[...] = jnp.zeros_like(lower_all)
+        corner_all[...] = jnp.zeros_like(corner_all)
+        above_first[...] = jnp.zeros_like(above_first)
+        above_second[...] = jnp.zeros_like(above_second)
+
+    @pl.when(jnp.logical_not(has_down))
+    def _():
+        below_first[...] = jnp.zeros_like(below_first)
+        below_second[...] = jnp.zeros_like(below_second)
+
+    pl.semaphore_wait(barrier, 1 + has_up.astype(jnp.int32) + has_down.astype(jnp.int32))
 
     sends = []
 
-    def send(src, dst, peer):
-        at = len(sends)
-        copy = pltpu.make_async_remote_copy(
-            src_ref=src,
-            dst_ref=dst,
-            send_sem=send_sem.at[at],
-            recv_sem=recv_sem.at[at],
-            device_id=peer,
-            device_id_type=MESH,
-        )
-        copy.start()
-        sends.append(copy)
-        return copy
+    class Send:
+        def __init__(self, src, dst, peer, given, taken):
+            at = len(sends)
+            self.given, self.taken = given, taken
+            self.copy = pltpu.make_async_remote_copy(
+                src_ref=src,
+                dst_ref=dst,
+                send_sem=send_sem.at[at],
+                recv_sem=recv_sem.at[at],
+                device_id=peer,
+                device_id_type=MESH,
+            )
+            self.on(given, self.copy.start)
+            sends.append(self)
+
+        def on(self, condition, action):
+            if condition is None:
+                action()
+            else:
+                pl.when(condition)(lambda: action())
+
+        def wait_recv(self):
+            self.on(self.taken, self.copy.wait_recv)
+
+        def wait_send(self):
+            self.on(self.given, self.copy.wait_send)
+
+    def send(src, dst, to):
+        if to == "mate":
+            return Send(src, dst, mate, None, None)
+        if to == "down":
+            return Send(src, dst, down, has_down, has_up)
+        return Send(src, dst, up, has_up, has_down)
 
     def send_down_first(k):
         return send(
-            panel.at[pl.ds(3 * nb, nb), pl.ds(k * chunk, chunk)], above_first.at[k], down
+            panel.at[pl.ds(3 * nb, nb), pl.ds(k * chunk, chunk)], above_first.at[k], "down"
         )
 
     vec_from_mate = {}
-    vec_from_mate[0] = send(border_vecs.at[0, 0], vec_border.at[0, mine], mate)
+    vec_from_mate[0] = send(border_vecs.at[0, 0], vec_border.at[0, mine], "mate")
     down_first = [send_down_first(0)]
     up_first = [
-        send(panel.at[pl.ds(0, nb), pl.ds(k * chunk, chunk)], below_first.at[k], up)
+        send(panel.at[pl.ds(0, nb), pl.ds(k * chunk, chunk)], below_first.at[k], "up")
         for k in range(CHUNKS)
     ]
-    vec_from_mate[2] = send(border_vecs.at[0, 2], vec_border.at[2, mine], mate)
+    vec_from_mate[2] = send(border_vecs.at[0, 2], vec_border.at[2, mine], "mate")
     down_first.append(send_down_first(1))
-    inner_from_mate = send(inner_vecs.at[0], vec_inner.at[:, mine], mate)
-    vec_from_mate[1] = send(border_vecs.at[0, 1], vec_border.at[1, mine], mate)
-    vec_from_mate[3] = send(border_vecs.at[0, 3], vec_border.at[3, mine], mate)
+    inner_from_mate = send(inner_vecs.at[0], vec_inner.at[:, mine], "mate")
+    vec_from_mate[1] = send(border_vecs.at[0, 1], vec_border.at[1, mine], "mate")
+    vec_from_mate[3] = send(border_vecs.at[0, 3], vec_border.at[3, mine], "mate")
 
     def build(slot, vectors, factor, scale):
         v = halves(vectors)
@@ -136,8 +180,8 @@
         return q
 
     def active(s):
-        start = group_start[s]
-        span = group_span[s]
+        start = start_ref[s]
+        span = span_ref[s]
         return ((row >= start) & (row < start + span)).astype(F32)
 
     def build_border(s):
@@ -146,6 +190,8 @@
     for copy in load_border:
         copy.wait()
     load_fac_border.wait()
+    load_start.wait()
+    load_span.wait()
 
     vec_from_mate[0].wait_recv()
     q = build_border(0)
@@ -153,8 +199,8 @@
     vec_from_mate[2].wait_recv()
     q = build_border(2)
     corner_send[...] = q[nb:, nb:]
-    lower_down = send(lower_send.at[mine_half], lower_all.at[mine_half], down)
-    corner_down = send(corner_send.at[mine_half], corner_all.at[mine_half], down)
+    lower_down = send(lower_send.at[mine_half], lower_all.at[mine_half], "down")
+    corner_down = send(corner_send.at[mine_half], corner_all.at[mine_half], "down")
     for k in range(2, CHUNKS):
         down_first.append(send_down_first(k))
 
@@ -177,10 +223,7 @@
     up_second, down_second = [], []
 
     def lower_side(k):
-        if k == 0:
-            load_panel_wait(0)
-        else:
-            load_panel_wait(k)
+        load_panel[k].wait()
         state[k, nb : 3 * nb] = apply(0, state[k, nb : 3 * nb])
         up_first[k].wait_recv()
         last = state[k, 3 * nb :]
@@ -191,11 +234,8 @@
         state[k, 2 * nb :] = band
         share[k] = product(q_of(6, slice(nb, None), slice(0, nb)), halves(band[nb:]))
 
-    def load_panel_wait(k):
-        load_panel[k].wait()
-
     def send_share(k):
-        down_second.append(send(share.at[k], above_second.at[k], down))
+        down_second.append(send(share.at[k], above_second.at[k], "down"))
 
     def upper_side(k):
         down_first[k].wait_recv()
@@ -208,17 +248,19 @@
         raise_buf[k] = band[:nb]
 
     def send_raise(k):
-        up_second.append(send(raise_buf.at[k], below_second.at[k], up))
+        up_second.append(send(raise_buf.at[k], below_second.at[k], "up"))
 
     def middle(k):
         state[k, nb : 3 * nb] = apply(2, state[k, nb : 3 * nb])
 
-    def finish(k):
+    def finish_upper(k):
         down_second[k].wait_recv()
         first = state[k, :nb]
         first = first - (product(halves(corner_all[...]), halves(first)) + above_second[k])
         band = jnp.concatenate([first, state[k, nb : 2 * nb]], axis=0)
         out[: 2 * nb, k * chunk : (k + 1) * chunk] = apply(3, band)
+
+    def finish_lower(k):
         up_second[k].wait_recv()
         last = state[k, 3 * nb :]
         band = jnp.concatenate([last, below_second[k]], axis=0)
@@ -231,8 +273,8 @@
     send_share(0)
     lower_down.wait_recv()
     corner_down.wait_recv()
-    lower_pair = send(lower_all.at[mine_half], lower_all.at[mine_half], mate)
-    corner_pair = send(corner_all.at[mine_half], corner_all.at[mine_half], mate)
+    lower_pair = send(lower_all.at[mine_half], lower_all.at[mine_half], "mate")
+    corner_pair = send(corner_all.at[mine_half], corner_all.at[mine_half], "mate")
     lower_pair.wait_recv()
     corner_pair.wait_recv()
     upper_side(0)
@@ -251,8 +293,11 @@
     send_raise(3)
     for k in range(1, CHUNKS):
         middle(k)
-    for k in range(CHUNKS):
-        finish(k)
+    finish_lower(0)
+    for k in range(1, CHUNKS):
+        finish_lower(k)
+        finish_upper(k - 1)
+    finish_upper(CHUNKS - 1)
     for copy in sends:
         copy.wait_send()
 
@@ -263,13 +308,12 @@
     chunk = width // CHUNKS
     steps = inner_factor.shape[1]
     vmem, dma = pltpu.VMEM, pltpu.SemaphoreType.DMA
-    anywhere = pl.BlockSpec(memory_space=pl.ANY)
-    scalars = pl.BlockSpec(memory_space=pltpu.SMEM)
+    anywhere = pl.BlockSpec(memory_space=pltpu.HBM)
     copies = 4 * CHUNKS + 5 + 4
     return pl.pallas_call(
         functools.partial(kernel, rows),
         out_shape=jax.ShapeDtypeStruct(panel.shape, F32),
-        in_specs=[anywhere] * 5 + [scalars] * 2,
+        in_specs=[anywhere] * 7,
         out_specs=pl.BlockSpec(memory_space=pltpu.VMEM),
         scratch_shapes=[
             vmem((CHUNKS, height, chunk), F32),
@@ -289,7 +333,9 @@
             vmem((CHUNKS, nb, chunk), F32),
             vmem((CHUNKS, nb, chunk), F32),
             vmem((CHUNKS, nb, chunk), F32),
-            dma((7 + CHUNKS,)),
+            pltpu.SMEM((steps,), jnp.int32),
+            pltpu.SMEM((steps,), jnp.int32),
+            dma((9 + CHUNKS,)),
             dma((copies,)),
             dma((copies,)),
         ],
@@ -297,7 +343,20 @@
             collective_id=0, has_side_effects=True, vmem_limit_bytes=48 * 2**20
         ),
         name="diamonds",
-    )(panel, inner_vecs, inner_factor, border_vecs, border_factor, group_start, group_span)
+    )(
+        *(
+            pltpu.with_memory_space_constraint(a, pltpu.HBM)
+            for a in (
+                panel,
+                inner_vecs,
+                inner_factor,
+                border_vecs,
+                border_factor,
+                group_start,
+                group_span,
+            )
+        )
+    )
 
 
 def solution(mesh):

time: 53.8 us -> 42.2 us (0.78)
  the two profiles are of different devices: /device:TPU:1 before, /device:TPU:48 now
where the time goes in v2:
time: 42.2 us; the launch traced here: 41.4 us
  Pallas kernels  40.1 us (95%)
  local copies, waits for them, and re-layouts  1.32 us (3%)
    pallas_call x1, Pallas kernels, local(): pl.pallas_call(functools.partial(kernel, rows), out_shape=jax.ShapeDtypeS...  40.1 us
    unnamed x1, local copies, waits for them, and re-layouts  1.32 us

profile of v2, /device:TPU:48, one launch (start us, length us, event | category | flops | bytes accessed | tf_op | source)
XLA Modules:
  0.0 41.4 jit_solution(16296343414456962667)
XLA Ops:
  0.0 40.1 %diamonds.1 = f32[512,1024]{1,0:T(8,128)S(1)} custom-call(f32[512,1024]{1,0:T(8,128)} %panel.1, f32[1,4,128,128]{3,2,1,0:T(8,128)} %inner_vecs.1, f32[1,4,128,128]{3,2,1,0:T(8,128)} %inner_factor.1, f32[1,4,128,128]{3,2,1,0:T(8,128)} %border_vecs.1, f32[1,4,128,128]{3,2,1,0:T(8,128)} %border_factor.1, s32[4]{0:T(128)} %group_start.1, s32[4]{0:T(128)} %group_span.1), custom_call_target="tpu_custom_call" | custom-call | tf_op jit(solution)/shard_map/diamonds/pallas_call | solution.py:313
  40.1 1.3 %copy.9 = f32[512,1024]{1,0:T(8,128)} copy(f32[512,1024]{1,0:T(8,128)S(1)} %diamonds.1) | data formatting | bytes 4194304

commit v3 on v2

v3 whole, which is shorter than its diff:
```python
import functools

import jax
import jax.numpy as jnp
from jax import lax
from jax.experimental import pallas as pl
from jax.experimental.pallas import tpu as pltpu
from jax.sharding import PartitionSpec as P

MESH = pl.DeviceIdType.MESH
F32 = jnp.float32
BF16 = jnp.bfloat16
CHUNKS = 4
EXTENT_Z = 8


def halves(value):
    high = value.astype(BF16)
    low = (value - high.astype(F32)).astype(BF16)
    return high, low


def product(a, b, dims=((1,), (0,))):
    def dot(left, right):
        return lax.dot_general(left, right, (dims, ((), ())), preferred_element_type=F32)

    return dot(a[0], b[0]) + (dot(a[0], b[1]) + dot(a[1], b[0]))


def both(*conditions):
    return functools.reduce(jnp.logical_and, conditions)


def on(condition, action):
    if condition is None:
        action()
    else:
        pl.when(condition)(lambda: action())


def kernel(
    rows,
    panel,
    inner_vecs,
    inner_factor,
    border_vecs,
    border_factor,
    group_start,
    group_span,
    out,
    state,
    vec_inner,
    vec_border,
    fac_inner,
    fac_border,
    q_high,
    q_low,
    lower_send,
    lower_all,
    corner_send,
    corner_all,
    above_first,
    below_first,
    above_second,
    below_second,
    share,
    raise_buf,
    start_ref,
    span_ref,
    load_sem,
    send_sem,
    recv_sem,
):
    row = lax.axis_index("row")
    col = lax.axis_index("col")
    height, width = panel.shape
    nb = height // 4
    chunk = width // CHUNKS
    half = nb // 2
    last = CHUNKS - 1
    z = lax.rem(row, EXTENT_Z)
    has_up, has_down = row > 0, row < rows - 1
    down = (jnp.minimum(row + 1, rows - 1), col)
    up = (jnp.maximum(row - 1, 0), col)
    mate = (row, 1 - col)
    top = z == 0
    mine = pl.ds(pl.multiple_of(col * nb, nb), nb)
    mine_half = pl.ds(pl.multiple_of(col * half, half), half)

    barrier = pltpu.get_barrier_semaphore()

    def greet(peer):
        pl.semaphore_signal(barrier, inc=1, device_id=peer, device_id_type=MESH)

    on(has_up, lambda: greet(up))
    on(has_down, lambda: greet(down))
    greet(mate)
    loads = []

    def load(src, dst):
        copy = pltpu.make_async_copy(src, dst, load_sem.at[len(loads)])
        copy.start()
        loads.append(copy)
        return copy

    load_border = load(border_vecs.at[0], vec_border.at[:, mine])
    load_fac_border = load(border_factor.at[0], fac_border)
    load_start = load(group_start, start_ref)
    load_span = load(group_span, span_ref)
    load_inner = load(inner_vecs.at[0], vec_inner.at[:, mine])
    load_fac_inner = load(inner_factor.at[0], fac_inner)
    load_panel = load(panel, state)

    @pl.when(jnp.logical_not(has_up))
    def _():
        lower_all[...] = jnp.zeros_like(lower_all)
        corner_all[...] = jnp.zeros_like(corner_all)
        above_first[...] = jnp.zeros_like(above_first)
        above_second[...] = jnp.zeros_like(above_second)

    @pl.when(jnp.logical_not(has_down))
    def _():
        below_first[...] = jnp.zeros_like(below_first)
        below_second[...] = jnp.zeros_like(below_second)

    def one(condition):
        return condition.astype(jnp.int32)

    pl.semaphore_wait(barrier, 1 + one(has_up) + one(has_down))

    sends = []

    class Send:
        def __init__(self, src, dst, peer, given, taken):
            self.given, self.taken = given, taken
            index = len(sends)
            self.copy = pltpu.make_async_remote_copy(
                src_ref=src,
                dst_ref=dst,
                send_sem=send_sem.at[index],
                recv_sem=recv_sem.at[index],
                device_id=peer,
                device_id_type=MESH,
            )
            sends.append(self)

        def start(self):
            on(self.given, self.copy.start)

        def wait_recv(self):
            on(self.taken, self.copy.wait_recv)

        def wait_send(self):
            on(self.given, self.copy.wait_send)

    def to_mate(src, dst):
        return Send(src, dst, mate, None, None)

    def to_down(src, dst, given=has_down, taken=has_up):
        return Send(src, dst, down, given, taken)

    def to_up(src, dst):
        return Send(src, dst, up, has_up, has_down)

    def border_rows(k, at_row, count):
        return panel.at[pl.ds(3 * nb + at_row, count), pl.ds(k * chunk, chunk)]

    down_first = [
        to_down(border_rows(k, 0, nb), above_first.at[k]) for k in range(CHUNKS)
    ]
    up_first = [
        to_up(panel.at[pl.ds(0, nb), pl.ds(k * chunk, chunk)], below_first.at[k])
        for k in range(CHUNKS)
    ]
    border_from_mate = [
        to_mate(border_vecs.at[0, pl.ds(s, n)], vec_border.at[pl.ds(s, n), mine])
        for s, n in ((0, 1), (1, 3))
    ]
    inner_from_mate = to_mate(inner_vecs.at[0], vec_inner.at[:, mine])
    lower_down = to_down(lower_send.at[mine_half], lower_all.at[mine_half])
    corner_down = to_down(corner_send.at[mine_half], corner_all.at[mine_half])
    lower_pair = to_mate(lower_all.at[mine_half], lower_all.at[mine_half])
    corner_pair = to_mate(corner_all.at[mine_half], corner_all.at[mine_half])
    down_second = [to_down(share.at[k], above_second.at[k]) for k in range(CHUNKS)]
    up_second = [to_up(raise_buf.at[k], below_second.at[k]) for k in range(CHUNKS)]

    down_first[0].start()
    border_from_mate[0].start()
    for copy in up_first:
        copy.start()
    border_from_mate[1].start()
    down_first[1].start()
    inner_from_mate.start()

    def build(slot, vectors, factor, scale):
        v = halves(vectors)
        w = halves(product(v, halves(factor)))
        q = product(w, v, ((1,), (1,)))
        if scale is not None:
            q = q * scale
        high, low = halves(q)
        q_high[slot] = high
        q_low[slot] = low
        return q

    def active(s):
        start = start_ref[s]
        span = span_ref[s]
        return ((row >= start) & (row < start + span)).astype(F32)

    def build_border(s):
        return build(4 + s, vec_border[s], fac_border[s], active(s))

    load_border.wait()
    load_fac_border.wait()
    load_start.wait()
    load_span.wait()

    border_from_mate[0].wait_recv()
    q = build_border(0)
    lower_send[...] = q[nb:]
    border_from_mate[1].wait_recv()
    q = build_border(2)
    corner_send[...] = q[nb:, nb:]
    lower_down.start()
    load_inner.wait()
    load_fac_inner.wait()
    inner_from_mate.wait_recv()
    build(0, vec_inner[0], fac_inner[0], None)
    corner_down.start()
    for copy in down_first[2:]:
        copy.start()

    build_border(1)
    for slot in (1, 2, 3):
        build(slot, vec_inner[slot], fac_inner[slot], None)
    build_border(3)

    def q_of(slot, r=slice(None), c=slice(None)):
        return q_high[slot, r, c], q_low[slot, r, c]

    def apply(slot, band):
        return band - product(q_of(slot), halves(band))

    load_panel.wait()

    def span_of(k):
        return slice(k * chunk, (k + 1) * chunk)

    def lower_side(k):
        state[nb : 3 * nb, span_of(k)] = apply(0, state[nb : 3 * nb, span_of(k)])
        up_first[k].wait_recv()
        end = state[3 * nb :, span_of(k)]
        band = jnp.concatenate([end, below_first[k]], axis=0)
        end = end - product(q_of(4, slice(0, nb)), halves(band))
        band = jnp.concatenate([state[2 * nb : 3 * nb, span_of(k)], end], axis=0)
        band = apply(5, band)
        share[k] = product(q_of(6, slice(nb, None), slice(0, nb)), halves(band[nb:]))
        state[2 * nb :, span_of(k)] = band

    def upper_side(k):
        down_first[k].wait_recv()
        first = state[:nb, span_of(k)]
        band = jnp.concatenate([above_first[k], first], axis=0)
        first = first - product(halves(lower_all[...]), halves(band))
        band = jnp.concatenate([first, state[nb : 2 * nb, span_of(k)]], axis=0)
        band = apply(1, band)
        raise_buf[k] = band[:nb]
        state[: 2 * nb, span_of(k)] = band

    def middle(k):
        state[nb : 3 * nb, span_of(k)] = apply(2, state[nb : 3 * nb, span_of(k)])
        first = state[:nb, span_of(k)]
        state[:nb, span_of(k)] = first - product(halves(corner_all[...]), halves(first))

    def finish_upper(k):
        down_second[k].wait_recv()
        first = state[:nb, span_of(k)] - above_second[k]
        band = jnp.concatenate([first, state[nb : 2 * nb, span_of(k)]], axis=0)
        out[: 2 * nb, span_of(k)] = apply(3, band)

    def finish_lower(k):
        up_second[k].wait_recv()
        end = state[3 * nb :, span_of(k)]
        band = jnp.concatenate([end, below_second[k]], axis=0)
        end = end - product(q_of(6, slice(0, nb)), halves(band))
        band = jnp.concatenate([state[2 * nb : 3 * nb, span_of(k)], end], axis=0)
        out[2 * nb :, span_of(k)] = apply(7, band)

    def weights():
        lower_down.wait_recv()
        lower_pair.start()
        corner_down.wait_recv()
        corner_pair.start()
        lower_pair.wait_recv()
        corner_pair.wait_recv()

    def sent_down(k):
        down_second[k].start()

    def sent_up(k):
        up_second[k].start()

    def early():
        for k in range(CHUNKS):
            lower_side(k)
            sent_down(k)
        weights()
        for k in range(CHUNKS):
            upper_side(k)
            sent_up(k)

    def usual():
        for k in range(CHUNKS):
            lower_side(k)
            sent_down(k)
            if k == 0:
                weights()
            upper_side(k)
            sent_up(k)

    pl.when(top)(early)
    pl.when(jnp.logical_not(top))(usual)
    for k in range(CHUNKS):
        middle(k)
    finish_lower(0)
    for k in range(1, CHUNKS):
        finish_lower(k)
        finish_upper(k - 1)
    finish_upper(last)
    for copy in sends:
        copy.wait_send()


def local(panel, inner_vecs, inner_factor, border_vecs, border_factor, group_start, group_span, *, rows):
    height, width = panel.shape
    nb = height // 4
    chunk = width // CHUNKS
    steps = inner_factor.shape[1]
    vmem, dma = pltpu.VMEM, pltpu.SemaphoreType.DMA
    anywhere = pl.BlockSpec(memory_space=pl.ANY)
    copies = 4 * CHUNKS + 7
    operands = (
        panel,
        inner_vecs,
        inner_factor,
        border_vecs,
        border_factor,
        group_start,
        group_span,
    )
    result = pl.pallas_call(
        functools.partial(kernel, rows),
        out_shape=jax.ShapeDtypeStruct(panel.shape, F32),
        in_specs=[pl.BlockSpec(memory_space=pltpu.HBM)] * 7,
        out_specs=pl.BlockSpec(memory_space=pltpu.VMEM),
        scratch_shapes=[
            vmem((height, width), F32),
            vmem((steps, 2 * nb, nb), F32),
            vmem((steps, 2 * nb, nb), F32),
            vmem((steps, nb, nb), F32),
            vmem((steps, nb, nb), F32),
            vmem((2 * steps, 2 * nb, 2 * nb), BF16),
            vmem((2 * steps, 2 * nb, 2 * nb), BF16),
            vmem((nb, 2 * nb), F32),
            vmem((nb, 2 * nb), F32),
            vmem((nb, nb), F32),
            vmem((nb, nb), F32),
            vmem((CHUNKS, nb, chunk), F32),
            vmem((CHUNKS, nb, chunk), F32),
            vmem((CHUNKS, nb, chunk), F32),
            vmem((CHUNKS, nb, chunk), F32),
            vmem((CHUNKS, nb, chunk), F32),
            vmem((CHUNKS, nb, chunk), F32),
            pltpu.SMEM((steps,), jnp.int32),
            pltpu.SMEM((steps,), jnp.int32),
            dma((7,)),
            dma((copies,)),
            dma((copies,)),
        ],
        compiler_params=pltpu.CompilerParams(
            collective_id=0, has_side_effects=True, vmem_limit_bytes=48 * 2**20
        ),
        name="diamonds",
    )(*(pltpu.with_memory_space_constraint(a, pltpu.HBM) for a in operands))
    return result


def solution(mesh):
    placed = (
        P("row", "col"),
        P("row", None, "col", None),
        P("row", None, None, None),
        P("row", None, "col", None),
        P("row", None, None, None),
        P(),
        P(),
    )
    return jax.shard_map(
        functools.partial(local, rows=mesh.shape["row"]),
        mesh=mesh,
        in_specs=placed,
        out_specs=P("row", "col"),
        check_vma=False,
    )
```

time: 42.2 us -> 41.2 us (0.976); the launches traced: 41.4 us -> 41.1 us
  no operation moved by 1% of the time
where the time goes in v3:
time: 41.2 us; the launch traced here: 41.1 us
  Pallas kernels  39.8 us (97%)
  local copies, waits for them, and re-layouts  1.32 us (3%)
    pallas_call x1, Pallas kernels, local(): pl.pallas_call(functools.partial(kernel, rows), out_shape=jax.ShapeDtypeS...  39.8 us
    unnamed x1, local copies, waits for them, and re-layouts  1.32 us

profile of v3, /device:TPU:48, one launch (start us, length us, event | category | flops | bytes accessed | tf_op | source)
XLA Modules:
  0.0 41.1 jit_solution(2323032057495205178)
XLA Ops:
  0.0 39.8 %diamonds.1 = f32[512,1024]{1,0:T(8,128)S(1)} custom-call(f32[512,1024]{1,0:T(8,128)} %panel.1, f32[1,4,128,128]{3,2,1,0:T(8,128)} %inner_vecs.1, f32[1,4,128,128]{3,2,1,0:T(8,128)} %inner_factor.1, f32[1,4,128,128]{3,2,1,0:T(8,128)} %border_vecs.1, f32[1,4,128,128]{3,2,1,0:T(8,128)} %border_factor.1, s32[4]{0:T(128)} %group_start.1, s32[4]{0:T(128)} %group_span.1), custom_call_target="tpu_custom_call" | custom-call | tf_op jit(solution)/shard_map/diamonds/pallas_call | solution.py:352
  39.8 1.3 %copy.9 = f32[512,1024]{1,0:T(8,128)} copy(f32[512,1024]{1,0:T(8,128)S(1)} %diamonds.1) | data formatting | bytes 4194304

commit v4 on v3

--- a/solution.py
+++ b/solution.py
@@ -189,27 +189,33 @@
     for copy in up_first:
         copy.start()
     border_from_mate[1].start()
-    down_first[1].start()
     inner_from_mate.start()
 
-    def build(slot, vectors, factor, scale):
+    def build(slot, vectors, factor, scale, keep=None):
         v = halves(vectors)
         w = halves(product(v, halves(factor)))
         q = product(w, v, ((1,), (1,)))
         if scale is not None:
             q = q * scale
+        if keep is not None:
+            keep(q)
         high, low = halves(q)
         q_high[slot] = high
         q_low[slot] = low
-        return q
 
     def active(s):
         start = start_ref[s]
         span = span_ref[s]
         return ((row >= start) & (row < start + span)).astype(F32)
 
-    def build_border(s):
-        return build(4 + s, vec_border[s], fac_border[s], active(s))
+    def build_border(s, keep=None):
+        build(4 + s, vec_border[s], fac_border[s], active(s), keep)
+
+    def keep_lower(q):
+        lower_send[...] = q[nb:]
+
+    def keep_corner(q):
+        corner_send[...] = q[nb:, nb:]
 
     load_border.wait()
     load_fac_border.wait()
@@ -217,19 +223,18 @@
     load_span.wait()
 
     border_from_mate[0].wait_recv()
-    q = build_border(0)
-    lower_send[...] = q[nb:]
+    build_border(0, keep_lower)
+    lower_down.start()
+    down_first[1].start()
     border_from_mate[1].wait_recv()
-    q = build_border(2)
-    corner_send[...] = q[nb:, nb:]
-    lower_down.start()
+    build_border(2, keep_corner)
+    corner_down.start()
+    for copy in down_first[2:]:
+        copy.start()
     load_inner.wait()
     load_fac_inner.wait()
     inner_from_mate.wait_recv()
     build(0, vec_inner[0], fac_inner[0], None)
-    corner_down.start()
-    for copy in down_first[2:]:
-        copy.start()
 
     build_border(1)
     for slot in (1, 2, 3):

time: 41.2 us -> 41.2 us (level)
  no operation moved by 1% of the time
where the time goes in v4:
time: 41.2 us; the launch traced here: 41.1 us
  Pallas kernels  39.8 us (97%)
  local copies, waits for them, and re-layouts  1.32 us (3%)
    pallas_call x1, Pallas kernels, local(): pl.pallas_call(functools.partial(kernel, rows), out_shape=jax.ShapeDtypeS...  39.8 us
    unnamed x1, local copies, waits for them, and re-layouts  1.32 us

profile of v4, /device:TPU:48, one launch (start us, length us, event | category | flops | bytes accessed | tf_op | source)
XLA Modules:
  0.0 41.1 jit_solution(10128696719159441874)
XLA Ops:
  0.0 39.8 %diamonds.1 = f32[512,1024]{1,0:T(8,128)S(1)} custom-call(f32[512,1024]{1,0:T(8,128)} %panel.1, f32[1,4,128,128]{3,2,1,0:T(8,128)} %inner_vecs.1, f32[1,4,128,128]{3,2,1,0:T(8,128)} %inner_factor.1, f32[1,4,128,128]{3,2,1,0:T(8,128)} %border_vecs.1, f32[1,4,128,128]{3,2,1,0:T(8,128)} %border_factor.1, s32[4]{0:T(128)} %group_start.1, s32[4]{0:T(128)} %group_span.1), custom_call_target="tpu_custom_call" | custom-call | tf_op jit(solution)/shard_map/diamonds/pallas_call | solution.py:357
  39.8 1.3 %copy.9 = f32[512,1024]{1,0:T(8,128)} copy(f32[512,1024]{1,0:T(8,128)S(1)} %diamonds.1) | data formatting | bytes 4194304
